TPU v7x, 256 devices: a whole 4x4x8 slice. The times are simulated.
256 devices in a mesh: ctx: 16 (over y, x), exp: 16 (over z, core).
Axes of the slice: x: 4, y: 4, z: 8, core: 2. Of those that a mesh axis runs over, the one named last changes fastest.
Arguments:
- tokens: bfloat16 [2048, 4096], P('ctx', 'exp'), may hold values from -6 to 6
- input_weight: bfloat16 [4096, 8192], P('ctx', 'exp'), may hold values from -0.09375 to 0.09375
- gate_weight: bfloat16 [4096, 8192], P('ctx', 'exp'), may hold values from -0.09375 to 0.09375
- conv_weight: float32 [4, 8192], P(None, 'exp'), may hold values from -3 to 3
- conv_bias: float32 [8192], P('exp'), may hold values from -3 to 3
- state_weight: bfloat16 [8192, 32], P('exp'), may hold values from -0.0078125 to 0.0078125
- step_size: float32 [2048, 8192], P('ctx', 'exp'), may hold values from 0 to 1, as said below
- skip_gain: float32 [8192], P('exp'), may hold values from 0.5 to 2
- output_weight: bfloat16 [8192, 4096], P('exp', 'ctx'), may hold values from -0.0625 to 0.0625
- norm_gain: float32 [4096], replicated, may hold values from 0.1 to 1.9
- router_weight: bfloat16 [4096, 16], replicated, may hold values from -0.09375 to 0.09375
- expert_gate: bfloat16 [16, 7168, 4096], P('exp', 'ctx'), may hold values from -0.09375 to 0.09375
- expert_up: bfloat16 [16, 7168, 4096], P('exp', 'ctx'), may hold values from -0.09375 to 0.09375
- expert_down: bfloat16 [16, 7168, 4096], P('exp', 'ctx'), may hold values from -0.0625 to 0.0625
- expert_ids: int32 [2048, 2], P(('ctx', 'exp')), may hold values from 0 to 15, all different within a row; in each aligned block of 8 rows (0 to 7, 8 to 15, ...) at most 2 rows name the same one
Outputs:
- layer_out: bfloat16 [2048, 4096], P(('ctx', 'exp'))
Inputs may be any that keep to these rules, and one draw needn't show every extreme that they name: `expert_ids`: each token names 2 different experts; in each aligned block of 8 tokens no expert is named by more than 2 tokens. `step_size`: a positive rate for each token and channel.
All inputs are finite; a program needn't handle non-finite values.
Results may differ from a plain program's by a relative error of at most 0.028.
Values may be sent and summed in bfloat16 or wider, within the bound.
A program may use at most 128 MiB of HBM per device.

v0:
```python
import jax
import jax.numpy as jnp
from jax import lax
from jax.sharding import PartitionSpec as P

STATE = 16
CONV = 4
TOP = 2
CAP = 2
precise = lax.Precision.HIGHEST


def shifted(shard, axis, by):
    devices = lax.axis_size(axis)
    pairs = [(i, i + by) for i in range(devices) if 0 <= i + by < devices]
    return lax.ppermute(shard, axis, pairs)


def running_sum(values):
    length = values.shape[0]
    lower = jnp.tril(jnp.ones((length, length), jnp.float32))
    return jnp.dot(lower, values, precision=precise)


def causal_part(scores, decay_block, input_block):
    length = decay_block.shape[0]
    causal = (jnp.arange(length)[:, None] >= jnp.arange(length)[None, :])[:, :, None]
    distance = decay_block[:, None, :] - decay_block[None, :, :]
    weight = jnp.where(causal, jnp.exp(-jnp.where(causal, distance, 0.0)), 0.0)
    return jnp.einsum("ts,tsc,sc->tc", scores, weight, input_block, precision=precise)


def local(
    tokens,
    input_weight,
    gate_weight,
    conv_weight,
    conv_bias,
    state_weight,
    step_size,
    skip_gain,
    output_weight,
    norm_gain,
    router_weight,
    expert_gate,
    expert_up,
    expert_down,
    expert_ids,
):
    whole_stretch = lax.all_gather(tokens, "exp", axis=1, tiled=True)
    stretch_rows = whole_stretch.shape[0]
    inner_width = input_weight.shape[1]
    inner_x = jnp.dot(
        whole_stretch,
        lax.all_gather(input_weight, "ctx", axis=0, tiled=True),
        preferred_element_type=jnp.float32,
    )
    inner_z = jnp.dot(
        whole_stretch,
        lax.all_gather(gate_weight, "ctx", axis=0, tiled=True),
        preferred_element_type=jnp.float32,
    )
    inner_x = inner_x.astype(jnp.bfloat16)
    inner_z = inner_z.astype(jnp.bfloat16)
    earlier_rows = shifted(inner_x[stretch_rows - (CONV - 1) :], "ctx", 1)
    extended = jnp.concatenate([earlier_rows, inner_x], 0).astype(jnp.float32)
    filtered = jnp.broadcast_to(conv_bias[None, :], (stretch_rows, inner_width))
    for offset in range(CONV):
        filtered = (
            filtered + conv_weight[offset][None, :] * extended[offset : offset + stretch_rows]
        )
    mixer_in = jax.nn.silu(filtered).astype(jnp.bfloat16)
    mixer_wide = mixer_in.astype(jnp.float32)
    projections = lax.psum(
        jnp.dot(mixer_in, state_weight, preferred_element_type=jnp.float32), "exp"
    )
    input_gain = projections[:, :STATE]
    readout = projections[:, STATE:]
    cumulative = running_sum(step_size)
    scores = jnp.dot(readout, input_gain.T, precision=precise)
    block_width = 128
    block_count = inner_width // block_width
    decay_blocks = cumulative.reshape(stretch_rows, block_count, block_width).transpose(1, 0, 2)
    incoming_slabs = mixer_wide.reshape(stretch_rows, block_count, block_width).transpose(1, 0, 2)
    inside = lax.map(
        lambda paired: causal_part(scores, paired[0], paired[1]), (decay_blocks, incoming_slabs)
    )
    inside = inside.transpose(1, 0, 2).reshape(stretch_rows, inner_width)
    total_decay = cumulative[stretch_rows - 1]
    tail_weight = jnp.exp(-(total_decay[None, :] - cumulative)) * mixer_wide
    local_end = jnp.dot(tail_weight.T, input_gain, precision=precise)
    stretch_keep = jnp.exp(-total_decay)

    def relay_step(turn_index, received):
        leaving = stretch_keep[:, None] * received + local_end
        return shifted(leaving, "ctx", 1)

    entering = lax.fori_loop(0, lax.axis_size("ctx") - 1, relay_step, jnp.zeros_like(local_end))
    carried = jnp.exp(-cumulative) * jnp.dot(readout, entering.T, precision=precise)
    mixed_state = (inside + carried + skip_gain[None, :] * mixer_wide) * jax.nn.silu(
        inner_z.astype(jnp.float32)
    )
    blender_result = mixed_state.astype(jnp.bfloat16)
    row_count = expert_ids.shape[0]
    start_row = lax.axis_index("exp") * row_count
    own_tokens = lax.dynamic_slice_in_dim(whole_stretch, start_row, row_count, 0)
    out_whole = lax.all_gather(output_weight, "ctx", axis=1, tiled=True)
    projected = lax.psum_scatter(
        jnp.dot(blender_result, out_whole, preferred_element_type=jnp.float32).astype(jnp.bfloat16),
        "exp",
        scatter_dimension=0,
        tiled=True,
    ).astype(jnp.float32)
    residual = (own_tokens.astype(jnp.float32) + projected).astype(jnp.bfloat16)
    stream = residual.astype(jnp.float32)
    normed = (
        stream
        * lax.rsqrt(jnp.mean(stream * stream, -1, keepdims=True) + 1e-05)
        * norm_gain[None, :]
    ).astype(jnp.bfloat16)
    logits = jnp.dot(normed, router_weight, preferred_element_type=jnp.float32)
    experts = router_weight.shape[1]
    expert_range = jnp.arange(experts, dtype=jnp.int32)
    chosen = expert_ids[:, :, None] == expert_range[None, None, :]
    selected_entry = jnp.sum(jnp.where(chosen, logits[:, None, :], 0.0), -1)
    shares = jax.nn.sigmoid(selected_entry - selected_entry[:, ::-1])
    flat_hits = chosen.reshape(row_count * TOP, experts).astype(jnp.int32)
    earlier_hits = jnp.dot(
        jnp.tril(jnp.ones((row_count * TOP, row_count * TOP), jnp.float32), -1),
        flat_hits.astype(jnp.float32),
        precision=precise,
    ).astype(jnp.int32)
    slot_index = jnp.sum(earlier_hits * flat_hits, -1)
    target = expert_ids.reshape(-1) * CAP + slot_index
    placed = target[:, None] == jnp.arange(experts * CAP, dtype=jnp.int32)[None, :]
    placed = placed.reshape(row_count, TOP, experts * CAP)
    selector = jnp.any(placed, 1).astype(jnp.bfloat16)
    outgoing = lax.dot_general(
        selector, normed, (((0,), (0,)), ((), ())), preferred_element_type=jnp.float32
    ).astype(jnp.bfloat16)
    outgoing = outgoing.reshape(experts, CAP, -1)
    arrived = lax.all_to_all(outgoing, "exp", split_axis=0, concat_axis=0, tiled=True)
    arrived = arrived.reshape(-1, arrived.shape[2])
    gate_part = expert_gate[0]
    up_part = expert_up[0]
    down_part = expert_down[0]
    shard_rows = lax.all_gather(arrived, "ctx", axis=0, tiled=True)
    gate_value = lax.dot_general(
        shard_rows, gate_part, (((1,), (1,)), ((), ())), preferred_element_type=jnp.float32
    )
    up_value = lax.dot_general(
        shard_rows, up_part, (((1,), (1,)), ((), ())), preferred_element_type=jnp.float32
    )
    hidden = (jax.nn.silu(gate_value) * up_value).astype(jnp.bfloat16)
    partial_out = jnp.dot(hidden, down_part, preferred_element_type=jnp.float32)
    finished = lax.psum_scatter(
        partial_out.astype(jnp.bfloat16), "ctx", scatter_dimension=0, tiled=True
    )
    returned = lax.all_to_all(
        finished.reshape(experts, CAP, -1), "exp", split_axis=0, concat_axis=0, tiled=True
    )
    returned = returned.reshape(experts * CAP, -1).astype(jnp.float32)
    combine = jnp.sum(jnp.where(placed, shares[:, :, None], 0.0), 1)
    moe_out = jnp.dot(combine, returned, precision=precise)
    return (stream + moe_out).astype(jnp.bfloat16)


def solution(mesh):
    in_specs = (
        P("ctx", "exp"),
        P("ctx", "exp"),
        P("ctx", "exp"),
        P(None, "exp"),
        P("exp"),
        P("exp", None),
        P("ctx", "exp"),
        P("exp"),
        P("exp", "ctx"),
        P(),
        P(),
        P("exp", "ctx", None),
        P("exp", "ctx", None),
        P("exp", "ctx", None),
        P(("ctx", "exp"), None),
    )
    out_specs = P(("ctx", "exp"), None)
    return jax.shard_map(local, mesh=mesh, in_specs=in_specs, out_specs=out_specs, check_vma=False)
```

profile of v0, /device:TPU:1, one launch (start us, length us, event | category | flops | bytes accessed | tf_op | source)
XLA Modules:
  0.0 636.4 jit_solution(114218375562185634)
XLA Ops:
  10.6 40.3 %all-gather.6.cloned.1.call-done = bf16[128,4096]{1,0:T(8,128)(2,1)} async-done(((bf16[128,256]{1,0:T(8,128)(2,1)}), bf16[128,4096]{1,0:T(8,128)(2,1)}) %all-gather.6.cloned.1.call-update) | async-done | bytes 1048592 | tf_op jit(solution)/shard_map/all_gather | solution.py:50
  51.0 57.7 %all-gather.8.cloned.1.call-done = bf16[4096,512]{1,0:T(8,128)(2,1)} async-done(((bf16[256,512]{1,0:T(8,128)(2,1)}), bf16[4096,512]{1,0:T(8,128)(2,1)}) %all-gather.8.cloned.1.call-update) | async-done | bytes 4194320 | tf_op jit(solution)/shard_map/all_gather | solution.py:55
  108.7 3.2 convolution_convert_fusion.4
  112.0 3.1 collective-permute-start.1
  115.1 52.4 %all-gather.10.cloned.1.call-done = bf16[4096,512]{1,0:T(8,128)(2,1)} async-done(((bf16[256,512]{1,0:T(8,128)(2,1)}), bf16[4096,512]{1,0:T(8,128)(2,1)}) %all-gather.10.cloned.1.call-update) | async-done | bytes 4194320 | tf_op jit(solution)/shard_map/all_gather | solution.py:60
  167.4 2.9 fusion.30
  170.7 46.7 %psum.7 = f32[128,32]{0,1:T(8,128)S(1)} all-reduce(f32[128,32]{0,1:T(8,128)S(1)} %fusion.70), channel_id=1, replica_groups=mesh['ctx'=16,'exp'=16] {'exp'}, use_global_device_ids=true, to_apply=%region_0.1 | all-reduce | flops 4096 | bytes 32768 | tf_op jit(solution)/shard_map/psum | solution.py:74
  218.1 39.1 %while.20 = (s32[]{:T(128)}, f32[4,128,128]{2,1,0:T(8,128)S(1)}, f32[4,128,128]{2,1,0:T(8,128)S(1)}, f32[4,128,128]{2,1,0:T(8,128)S(1)}, f32[128,128]{1,0:T(8,128)S(1)}, /*index=5*/s32[]{:T(128)}) while((s32[]{:T(128)}, f32[4,128,128]{2,1,0:T(8,128)S(1)}, f32[4,128,128]{2,1,0:T(8,128)S(1)}, f32[4,128,128]{2,1,0:T(8,128)S(1)}, ...), condition=%wide.region_2.3_spmd, body=%wide.region_1.2_spmd.sunk | while | flops 35667968 | bytes 688205 | solution.py:85
  218.1 9.7 %fusion.104 = f32[128,1,128]{2,1,0:T(1,128)S(1)} fusion(f32[128,128,1]{1,2,0:T(1,128)S(1)} %bitcast.89, f32[128,128]{1,0:T(8,128)S(1)} %get-tuple-element.140, f32[128,128]{1,0:T(8,128)S(1)} %get-tuple-element.141, pred[128,128]{1,0:T(8,128)(4,1)S(1)} %iota_compare_fusion.10), kind=kOutput, calls=%fused_computation.clone.1 | convolution fusion | flops 35651584 | bytes 278528 | tf_op jit(solution)/shard_map/while/body/eval_jaxpr/ts,tsc,sc->tc/dot_general | solution.py:30
  227.9 9.7 %fusion.104 = f32[128,1,128]{2,1,0:T(1,128)S(1)} fusion(f32[128,128,1]{1,2,0:T(1,128)S(1)} %bitcast.89, f32[128,128]{1,0:T(8,128)S(1)} %get-tuple-element.140, f32[128,128]{1,0:T(8,128)S(1)} %get-tuple-element.141, pred[128,128]{1,0:T(8,128)(4,1)S(1)} %iota_compare_fusion.10), kind=kOutput, calls=%fused_computation.clone.1 | convolution fusion | flops 35651584 | bytes 278528 | tf_op jit(solution)/shard_map/while/body/eval_jaxpr/ts,tsc,sc->tc/dot_general | solution.py:30
  237.6 9.7 %fusion.104 = f32[128,1,128]{2,1,0:T(1,128)S(1)} fusion(f32[128,128,1]{1,2,0:T(1,128)S(1)} %bitcast.89, f32[128,128]{1,0:T(8,128)S(1)} %get-tuple-element.140, f32[128,128]{1,0:T(8,128)S(1)} %get-tuple-element.141, pred[128,128]{1,0:T(8,128)(4,1)S(1)} %iota_compare_fusion.10), kind=kOutput, calls=%fused_computation.clone.1 | convolution fusion | flops 35651584 | bytes 278528 | tf_op jit(solution)/shard_map/while/body/eval_jaxpr/ts,tsc,sc->tc/dot_general | solution.py:30
  247.4 9.7 %fusion.104 = f32[128,1,128]{2,1,0:T(1,128)S(1)} fusion(f32[128,128,1]{1,2,0:T(1,128)S(1)} %bitcast.89, f32[128,128]{1,0:T(8,128)S(1)} %get-tuple-element.140, f32[128,128]{1,0:T(8,128)S(1)} %get-tuple-element.141, pred[128,128]{1,0:T(8,128)(4,1)S(1)} %iota_compare_fusion.10), kind=kOutput, calls=%fused_computation.clone.1 | convolution fusion | flops 35651584 | bytes 278528 | tf_op jit(solution)/shard_map/while/body/eval_jaxpr/ts,tsc,sc->tc/dot_general | solution.py:30
  257.1 90.6 %while.21 = (s32[]{:T(128)}, f32[512,16]{0,1:T(8,128)S(1)}, f32[512]{0:T(512)S(1)}, f32[512,16]{0,1:T(8,128)S(1)}, s32[]{:T(128)}) while((s32[]{:T(128)}, f32[512,16]{0,1:T(8,128)S(1)}, f32[512]{0:T(512)S(1)}, f32[512,16]{0,1:T(8,128)S(1)}, s32[]{:T(128)}) %tuple.40), condition=%wide.region_4.5_spmd, body=%wide.region_3.4_spmd.sunk | while | flops 16386 | bytes 231525 | solution.py:98
  257.2 2.7 collective-permute-start
  259.9 1.0 collective-permute-done
  260.9 3.6 collective-permute-start
  264.5 1.0 collective-permute-done
  265.5 3.6 collective-permute-start
  269.2 1.0 collective-permute-done
  270.2 4.0 collective-permute-start
  274.3 1.0 collective-permute-done
  275.3 3.7 collective-permute-start
  280.0 5.8 collective-permute-start
  286.8 5.7 collective-permute-start
  293.5 5.8 collective-permute-start
  300.3 5.8 collective-permute-start
  307.1 5.8 collective-permute-start
  312.8 1.0 collective-permute-done
  313.8 5.8 collective-permute-start
  319.6 1.0 collective-permute-done
  320.6 5.8 collective-permute-start
  326.4 1.2 collective-permute-done
  327.6 5.6 collective-permute-start
  333.1 1.0 collective-permute-done
  334.2 5.8 collective-permute-start
  339.9 1.0 collective-permute-done
  340.9 5.8 collective-permute-start
  346.7 1.0 collective-permute-done
  348.2 3.9 convolution_convert_fusion.1
  352.9 81.1 %reduce-scatter.3.cloned.1.call-done = bf16[8,4096]{1,0:T(8,128)(2,1)} async-done(((bf16[128,4096]{1,0:T(8,128)(2,1)}), bf16[8,4096]{1,0:T(8,128)(2,1)}) %reduce-scatter.3.cloned.1.call-update) | async-done | bytes 65552 | tf_op jit(solution)/shard_map/reduce_scatter | solution.py:108
  435.4 19.1 %all_to_all.10 = bf16[16,2,4096]{2,1,0:T(2,128)(2,1)S(1)} all-to-all(bf16[16,2,4096]{2,1,0:T(2,128)(2,1)S(1)} %reshape.74), channel_id=1, replica_groups=mesh['ctx'=16,'exp'=16] {'exp'}, dimensions={0} | all-to-all | bytes 524288 | tf_op jit(solution)/shard_map/all_to_all | solution.py:142
  455.6 53.0 %all-gather.14.cloned.1.call-done = bf16[512,4096]{1,0:T(8,128)(2,1)} async-done(((bf16[32,4096]{1,0:T(8,128)(2,1)}), bf16[512,4096]{1,0:T(8,128)(2,1)}) %all-gather.14.cloned.1.call-update) | async-done | bytes 4194320 | tf_op jit(solution)/shard_map/all_gather | solution.py:147
  508.6 5.4 fusion.18
  514.0 10.8 %convolution_convert_fusion = bf16[512,4096]{1,0:T(8,128)(2,1)} fusion(bf16[1,448,4096]{2,1,0:T(8,128)(2,1)} %param.32, bf16[512,4096]{1,0:T(8,128)(2,1)} %all-gather.14.cloned.1.call-done, bf16[1,448,4096]{2,1,0:T(8,128)(2,1)} %param.31, f32[512,448]{0,1:T(8,128)S(1)} %fusion.18), kind=kOutput, calls=%fused_computation.19 | convolution fusion | flops 3761569792 | bytes 16646144 | tf_op jit(solution)/shard_map/dot_general | solution.py:155
  524.8 80.9 %reduce-scatter.5.cloned.1.call-done = bf16[32,4096]{1,0:T(8,128)(2,1)} async-done(((bf16[512,4096]{1,0:T(8,128)(2,1)}), bf16[32,4096]{1,0:T(8,128)(2,1)}) %reduce-scatter.5.cloned.1.call-update) | async-done | bytes 262160 | tf_op jit(solution)/shard_map/reduce_scatter | solution.py:156
  605.7 1.8 reshape.76
  607.5 9.4 %all-to-all-start.1 = ((bf16[16,2,4096]{2,1,0:T(2,128)(2,1)}), bf16[16,2,4096]{2,1,0:T(2,128)(2,1)S(1)}, u32[]{:S(2)}, u32[]{:S(2)}) async-start(bf16[16,2,4096]{2,1,0:T(2,128)(2,1)} %reshape.76), calls=%async_computation.3 | async-start | bytes 524288 | tf_op jit(solution)/shard_map/all_to_all | solution.py:159
  617.4 11.2 %all-to-all-done.1 = bf16[16,2,4096]{2,1,0:T(2,128)(2,1)S(1)} async-done(((bf16[16,2,4096]{2,1,0:T(2,128)(2,1)}), bf16[16,2,4096]{2,1,0:T(2,128)(2,1)S(1)}, u32[]{:S(2)}, u32[]{:S(2)}) %all-to-all-start.1) | async-done | bytes 262176 | tf_op jit(solution)/shard_map/all_to_all | solution.py:159
  (98 shorter events, 15.5 us)
Async XLA Ops:
  6.5 3.7 copy-start
  6.5 44.5 %all-gather.6.cloned.1.call-start = ((), (), s32[]{:S(2)}) async-start(), calls=%async_computation.4 | async-start | bytes 1114112 | tf_op jit(solution)/shard_map/all_gather | solution.py:50
  7.3 101.4 %all-gather.8.cloned.1.call-start = ((), (), s32[]{:S(2)}) async-start(), calls=%async_computation.5 | async-start | bytes 4456448 | tf_op jit(solution)/shard_map/all_gather | solution.py:55
  8.0 159.4 %all-gather.10.cloned.1.call-start = ((), (), s32[]{:S(2)}) async-start(), calls=%async_computation.6 | async-start | bytes 4456448 | tf_op jit(solution)/shard_map/all_gather | solution.py:60
  8.7 339.5 %all-gather.12.cloned.1.call-start = ((), (), s32[]{:S(2)}) async-start(), calls=%async_computation.7 | async-start | bytes 4456448 | tf_op jit(solution)/shard_map/all_gather | solution.py:107
  9.3 424.6 %reduce-scatter.3.cloned.1.call-start = ((), (), s32[]{:S(2)}) async-start(), calls=%async_computation.8 | async-start | bytes 1114112 | tf_op jit(solution)/shard_map/reduce_scatter | solution.py:108
  51.0 116.5 %copy-start.1 = (bf16[128,4096]{1,0:T(8,128)(2,1)S(1)}, bf16[128,4096]{1,0:T(8,128)(2,1)}, u32[]{:S(2)}) copy-start(bf16[128,4096]{1,0:T(8,128)(2,1)} %all-gather.6.cloned.1.call-done) | copy-start | bytes 3145732
  111.9 58.5 %copy-start.5 = (f32[512]{0:T(512)S(1)}, f32[512]{0:T(512)}, u32[]{:S(2)}) copy-start(f32[512]{0:T(512)} %param.23) | copy-start | bytes 6148
  111.9 58.7 %copy-start.2 = (bf16[512,32]{0,1:T(8,128)(2,1)S(1)}, bf16[512,32]{0,1:T(8,128)(2,1)}, u32[]{:S(2)}) copy-start(bf16[512,32]{0,1:T(8,128)(2,1)} %param.24) | copy-start | bytes 98308
  112.0 58.4 %collective-permute-start.1 = (bf16[3,512]{1,0:T(4,128)(2,1)S(1)}, bf16[3,512]{1,0:T(4,128)(2,1)S(1)}, u32[]{:S(2)}, u32[]{:S(2)}) collective-permute-start(bf16[3,512]{1,0:T(4,128)(2,1)S(1)} %slice.48), channel_id=1, source_target_pairs={{0,16},{16,32},{32,48},{48,64},{64,80},{80,96},{96,112},{112,128},... | collective-permute-start | bytes 9224 | tf_op jit(solution)/shard_map/ppermute | solution.py:16
  218.1 129.7 %copy-start.7 = (f32[512]{0:T(512)S(1)}, f32[512]{0:T(512)}, u32[]{:S(2)}) copy-start(f32[512]{0:T(512)} %param.26) | copy-start | bytes 6148
  257.2 3.7 collective-permute-start
  260.9 4.7 collective-permute-start
  265.5 4.7 collective-permute-start
  270.2 5.1 collective-permute-start
  275.3 4.7 collective-permute-start
  280.0 6.9 %collective-permute-start = (f32[512,16]{0,1:T(8,128)S(1)}, f32[512,16]{0,1:T(8,128)S(1)}, u32[]{:S(2)}, u32[]{:S(2)}) collective-permute-start(f32[512,16]{0,1:T(8,128)S(1)} %multiply_add_fusion.3), channel_id=1, source_target_pairs={{0,16},{16,32},{32,48},{48,64},{64,80},{80,96},{96,112},{112,128},... | collective-permute-start | bytes 98312 | tf_op jit(solution)/shard_map/while/body/eval_jaxpr/ppermute | solution.py:16
  286.8 6.7 %collective-permute-start = (f32[512,16]{0,1:T(8,128)S(1)}, f32[512,16]{0,1:T(8,128)S(1)}, u32[]{:S(2)}, u32[]{:S(2)}) collective-permute-start(f32[512,16]{0,1:T(8,128)S(1)} %multiply_add_fusion.3), channel_id=1, source_target_pairs={{0,16},{16,32},{32,48},{48,64},{64,80},{80,96},{96,112},{112,128},... | collective-permute-start | bytes 98312 | tf_op jit(solution)/shard_map/while/body/eval_jaxpr/ppermute | solution.py:16
  293.5 6.8 %collective-permute-start = (f32[512,16]{0,1:T(8,128)S(1)}, f32[512,16]{0,1:T(8,128)S(1)}, u32[]{:S(2)}, u32[]{:S(2)}) collective-permute-start(f32[512,16]{0,1:T(8,128)S(1)} %multiply_add_fusion.3), channel_id=1, source_target_pairs={{0,16},{16,32},{32,48},{48,64},{64,80},{80,96},{96,112},{112,128},... | collective-permute-start | bytes 98312 | tf_op jit(solution)/shard_map/while/body/eval_jaxpr/ppermute | solution.py:16
  300.3 6.8 %collective-permute-start = (f32[512,16]{0,1:T(8,128)S(1)}, f32[512,16]{0,1:T(8,128)S(1)}, u32[]{:S(2)}, u32[]{:S(2)}) collective-permute-start(f32[512,16]{0,1:T(8,128)S(1)} %multiply_add_fusion.3), channel_id=1, source_target_pairs={{0,16},{16,32},{32,48},{48,64},{64,80},{80,96},{96,112},{112,128},... | collective-permute-start | bytes 98312 | tf_op jit(solution)/shard_map/while/body/eval_jaxpr/ppermute | solution.py:16
  307.1 6.8 %collective-permute-start = (f32[512,16]{0,1:T(8,128)S(1)}, f32[512,16]{0,1:T(8,128)S(1)}, u32[]{:S(2)}, u32[]{:S(2)}) collective-permute-start(f32[512,16]{0,1:T(8,128)S(1)} %multiply_add_fusion.3), channel_id=1, source_target_pairs={{0,16},{16,32},{32,48},{48,64},{64,80},{80,96},{96,112},{112,128},... | collective-permute-start | bytes 98312 | tf_op jit(solution)/shard_map/while/body/eval_jaxpr/ppermute | solution.py:16
  313.8 6.8 %collective-permute-start = (f32[512,16]{0,1:T(8,128)S(1)}, f32[512,16]{0,1:T(8,128)S(1)}, u32[]{:S(2)}, u32[]{:S(2)}) collective-permute-start(f32[512,16]{0,1:T(8,128)S(1)} %multiply_add_fusion.3), channel_id=1, source_target_pairs={{0,16},{16,32},{32,48},{48,64},{64,80},{80,96},{96,112},{112,128},... | collective-permute-start | bytes 98312 | tf_op jit(solution)/shard_map/while/body/eval_jaxpr/ppermute | solution.py:16
  320.6 6.9 %collective-permute-start = (f32[512,16]{0,1:T(8,128)S(1)}, f32[512,16]{0,1:T(8,128)S(1)}, u32[]{:S(2)}, u32[]{:S(2)}) collective-permute-start(f32[512,16]{0,1:T(8,128)S(1)} %multiply_add_fusion.3), channel_id=1, source_target_pairs={{0,16},{16,32},{32,48},{48,64},{64,80},{80,96},{96,112},{112,128},... | collective-permute-start | bytes 98312 | tf_op jit(solution)/shard_map/while/body/eval_jaxpr/ppermute | solution.py:16
  327.6 6.6 %collective-permute-start = (f32[512,16]{0,1:T(8,128)S(1)}, f32[512,16]{0,1:T(8,128)S(1)}, u32[]{:S(2)}, u32[]{:S(2)}) collective-permute-start(f32[512,16]{0,1:T(8,128)S(1)} %multiply_add_fusion.3), channel_id=1, source_target_pairs={{0,16},{16,32},{32,48},{48,64},{64,80},{80,96},{96,112},{112,128},... | collective-permute-start | bytes 98312 | tf_op jit(solution)/shard_map/while/body/eval_jaxpr/ppermute | solution.py:16
  334.2 6.8 %collective-permute-start = (f32[512,16]{0,1:T(8,128)S(1)}, f32[512,16]{0,1:T(8,128)S(1)}, u32[]{:S(2)}, u32[]{:S(2)}) collective-permute-start(f32[512,16]{0,1:T(8,128)S(1)} %multiply_add_fusion.3), channel_id=1, source_target_pairs={{0,16},{16,32},{32,48},{48,64},{64,80},{80,96},{96,112},{112,128},... | collective-permute-start | bytes 98312 | tf_op jit(solution)/shard_map/while/body/eval_jaxpr/ppermute | solution.py:16
  340.9 6.8 %collective-permute-start = (f32[512,16]{0,1:T(8,128)S(1)}, f32[512,16]{0,1:T(8,128)S(1)}, u32[]{:S(2)}, u32[]{:S(2)}) collective-permute-start(f32[512,16]{0,1:T(8,128)S(1)} %multiply_add_fusion.3), channel_id=1, source_target_pairs={{0,16},{16,32},{32,48},{48,64},{64,80},{80,96},{96,112},{112,128},... | collective-permute-start | bytes 98312 | tf_op jit(solution)/shard_map/while/body/eval_jaxpr/ppermute | solution.py:16
  347.7 4.5 copy-start.4
  347.7 87.2 %copy-start.3 = (f32[4096]{0:T(1024)S(1)}, f32[4096]{0:T(1024)}, u32[]{:S(2)}) copy-start(f32[4096]{0:T(1024)} %param.28) | copy-start | bytes 49156
  352.1 156.4 %all-gather.14.cloned.1.call-start = ((), (), s32[]{:S(2)}) async-start(), calls=%async_computation.9 | async-start | bytes 4456448 | tf_op jit(solution)/shard_map/all_gather | solution.py:147
  455.3 150.3 %reduce-scatter.5.cloned.1.call-start = ((), (), s32[]{:S(2)}) async-start(), calls=%async_computation.10 | async-start | bytes 4456448 | tf_op jit(solution)/shard_map/reduce_scatter | solution.py:156
  524.8 92.1 %copy-start.6 = (bf16[4096,16]{0,1:T(8,128)(2,1)S(1)}, bf16[4096,16]{0,1:T(8,128)(2,1)}, u32[]{:S(2)}) copy-start(bf16[4096,16]{0,1:T(8,128)(2,1)} %param.29) | copy-start | bytes 393220
  607.5 21.1 %all-to-all-start.1 = ((bf16[16,2,4096]{2,1,0:T(2,128)(2,1)}), bf16[16,2,4096]{2,1,0:T(2,128)(2,1)S(1)}, u32[]{:S(2)}, u32[]{:S(2)}) async-start(bf16[16,2,4096]{2,1,0:T(2,128)(2,1)} %reshape.76), calls=%async_computation.3 | async-start | bytes 524288 | tf_op jit(solution)/shard_map/all_to_all | solution.py:159
Sparse Core Ops, SparseCore 0:
  9.1 41.8 all-gather.5
  53.4 55.2 all-gather.7
  111.1 56.2 all-gather.9
  169.7 61.4 all-gather.11
  352.3 81.6 reduce-scatter.2
  455.4 53.0 all-gather.13
  524.9 80.7 reduce-scatter.4
where the time goes:
time: 637 us; the launch traced here: 636 us
  waiting for transfers between devices  394 us (62%)
  starting transfers between devices  87.9 us (14%)
  matrix products  68.1 us (11%)
  blocking collectives  65.7 us (10%)
  between operations  13.7 us (2%)
    reduce_scatter x1, waiting for transfers between devices, local(): lax.psum_scatter(jnp.dot(blender_result, out_whole, preferred_element_typ...  81.1 us
    reduce_scatter x1, waiting for transfers between devices, local(): lax.psum_scatter(partial_out.astype(jnp.bfloat16), 'ctx', scatter_dimensi...  80.9 us
    ppermute x16, starting transfers between devices, shifted(): return lax.ppermute(shard, axis, pairs)  78.2 us
    all_gather x1, waiting for transfers between devices, local(): lax.all_gather(input_weight, 'ctx', axis=0, tiled=True)  57.7 us
    all_gather x1, waiting for transfers between devices, local(): shard_rows = lax.all_gather(arrived, 'ctx', axis=0, tiled=True)  53 us
    all_gather x1, waiting for transfers between devices, local(): lax.all_gather(gate_weight, 'ctx', axis=0, tiled=True)  52.4 us
    psum x1, blocking collectives, local(): lax.psum(jnp.dot(mixer_in, state_weight, preferred_element_type=jnp.float...  46.7 us
    all_gather x1, waiting for transfers between devices, local(): whole_stretch = lax.all_gather(tokens, 'exp', axis=1, tiled=True)  40.3 us
  transfers between devices with their start and end apart: 24, of which 22 were waited for; matrix products, arithmetic and copies ran while one was open for 8% of the time, Pallas kernels for 0%

commit v1 on v0

--- a/solution.py
+++ b/solution.py
@@ -47,7 +47,9 @@
     expert_down,
     expert_ids,
 ):
-    whole_stretch = lax.all_gather(tokens, "exp", axis=1, tiled=True)
+    whole_stretch = jnp.concatenate(
+        lax.all_to_all(jnp.stack([tokens] * lax.axis_size("exp")), "exp", 0, 0), axis=1
+    )
     stretch_rows = whole_stretch.shape[0]
     inner_width = input_weight.shape[1]
     inner_x = jnp.dot(

time: 637 us -> 599 us (0.940)
  waiting for transfers between devices: 394 us -> 345 us
  starting transfers between devices: 87.9 us -> 97.5 us
    all_gather x1 -> x0, waiting for transfers between devices: 40.3 us -> none  [local(): whole_stretch = lax.all_gather(tokens, 'exp', axis=1, tiled=True)]
    all_gather x1, waiting for transfers between devices: 57.7 us -> 22.2 us  [local(): lax.all_gather(input_weight, 'ctx', axis=0, tiled=True)]
    all_to_all x0 -> x1, waiting for transfers between devices: none -> 26.7 us  [local(): lax.all_to_all(jnp.stack([tokens] * lax.axis_size('exp')), 'exp', 0, 0)]
    all_to_all x0 -> x1, starting transfers between devices: none -> 9.98 us  [local(): lax.all_to_all(jnp.stack([tokens] * lax.axis_size('exp')), 'exp', 0, 0)]
where the time goes in v1:
time: 599 us; the launch traced here: 598 us
  waiting for transfers between devices  345 us (58%)
  starting transfers between devices  97.5 us (16%)
  matrix products  67.7 us (11%)
  blocking collectives  66 us (11%)
  between operations  13.7 us (2%)
    reduce_scatter x1, waiting for transfers between devices, local(): lax.psum_scatter(jnp.dot(blender_result, out_whole, preferred_element_typ...  81.5 us
    reduce_scatter x1, waiting for transfers between devices, local(): lax.psum_scatter(partial_out.astype(jnp.bfloat16), 'ctx', scatter_dimensi...  80.9 us
    ppermute x16, starting transfers between devices, shifted(): return lax.ppermute(shard, axis, pairs)  77.8 us
    all_gather x1, waiting for transfers between devices, local(): shard_rows = lax.all_gather(arrived, 'ctx', axis=0, tiled=True)  52.9 us
    all_gather x1, waiting for transfers between devices, local(): lax.all_gather(gate_weight, 'ctx', axis=0, tiled=True)  52.7 us
    psum x1, blocking collectives, local(): lax.psum(jnp.dot(mixer_in, state_weight, preferred_element_type=jnp.float...  46.7 us
    dot_general x4, matrix products, causal_part(): jnp.einsum('ts,tsc,sc->tc', scores, weight, input_block, precision=precise)  38.7 us
    all_to_all x1, waiting for transfers between devices, local(): lax.all_to_all(jnp.stack([tokens] * lax.axis_size('exp')), 'exp', 0, 0)  26.7 us
  transfers between devices with their start and end apart: 24, of which 22 were waited for; matrix products, arithmetic and copies ran while one was open for 8% of the time, Pallas kernels for 0%

profile of v1, /device:TPU:1, one launch (start us, length us, event | category | flops | bytes accessed | tf_op | source)
XLA Modules:
  0.0 598.0 jit_solution(11785369126457917802)
XLA Ops:
  8.0 2.0 stack.2
  10.0 10.0 %all-to-all-start = ((bf16[16,128,256]{2,1,0:T(8,128)(2,1)}), bf16[16,128,256]{2,1,0:T(8,128)(2,1)S(1)}, u32[]{:S(2)}, u32[]{:S(2)}) async-start(bf16[16,128,256]{2,1,0:T(8,128)(2,1)} %stack.2), calls=%async_computation | async-start | bytes 2097152 | tf_op jit(solution)/shard_map/all_to_all | solution.py:51
  21.2 26.7 %all-to-all-done = bf16[16,128,256]{2,1,0:T(8,128)(2,1)S(1)} async-done(((bf16[16,128,256]{2,1,0:T(8,128)(2,1)}), bf16[16,128,256]{2,1,0:T(8,128)(2,1)S(1)}, u32[]{:S(2)}, u32[]{:S(2)}) %all-to-all-start) | async-done | bytes 1048608 | tf_op jit(solution)/shard_map/all_to_all | solution.py:51
  48.0 22.2 %all-gather.5.cloned.1.call-done = bf16[4096,512]{1,0:T(8,128)(2,1)} async-done(((bf16[256,512]{1,0:T(8,128)(2,1)}), bf16[4096,512]{1,0:T(8,128)(2,1)}) %all-gather.5.cloned.1.call-update) | async-done | bytes 4194320 | tf_op jit(solution)/shard_map/all_gather | solution.py:57
  70.2 2.9 convolution_convert_fusion.4
  73.1 3.1 collective-permute-start.1
  76.2 52.7 %all-gather.7.cloned.1.call-done = bf16[4096,512]{1,0:T(8,128)(2,1)} async-done(((bf16[256,512]{1,0:T(8,128)(2,1)}), bf16[4096,512]{1,0:T(8,128)(2,1)}) %all-gather.7.cloned.1.call-update) | async-done | bytes 4194320 | tf_op jit(solution)/shard_map/all_gather | solution.py:62
  128.9 2.9 fusion.30
  132.2 46.7 %psum.7 = f32[128,32]{0,1:T(8,128)S(1)} all-reduce(f32[128,32]{0,1:T(8,128)S(1)} %fusion.70), channel_id=1, replica_groups=mesh['ctx'=16,'exp'=16] {'exp'}, use_global_device_ids=true, to_apply=%region_0.1 | all-reduce | flops 4096 | bytes 32768 | tf_op jit(solution)/shard_map/psum | solution.py:76
  179.5 39.1 %while.20 = (s32[]{:T(128)}, f32[4,128,128]{2,1,0:T(8,128)S(1)}, f32[4,128,128]{2,1,0:T(8,128)S(1)}, f32[4,128,128]{2,1,0:T(8,128)S(1)}, f32[128,128]{1,0:T(8,128)S(1)}, /*index=5*/s32[]{:T(128)}) while((s32[]{:T(128)}, f32[4,128,128]{2,1,0:T(8,128)S(1)}, f32[4,128,128]{2,1,0:T(8,128)S(1)}, f32[4,128,128]{2,1,0:T(8,128)S(1)}, ...), condition=%wide.region_2.3_spmd, body=%wide.region_1.2_spmd.sunk | while | flops 35667968 | bytes 688205 | solution.py:87
  179.6 9.7 %fusion.104 = f32[128,1,128]{2,1,0:T(1,128)S(1)} fusion(f32[128,128,1]{1,2,0:T(1,128)S(1)} %bitcast.96, f32[128,128]{1,0:T(8,128)S(1)} %get-tuple-element.140, f32[128,128]{1,0:T(8,128)S(1)} %get-tuple-element.141, pred[128,128]{1,0:T(8,128)(4,1)S(1)} %iota_compare_fusion.10), kind=kOutput, calls=%fused_computation.clone.1 | convolution fusion | flops 35651584 | bytes 278528 | tf_op jit(solution)/shard_map/while/body/eval_jaxpr/ts,tsc,sc->tc/dot_general | solution.py:30
  189.4 9.7 %fusion.104 = f32[128,1,128]{2,1,0:T(1,128)S(1)} fusion(f32[128,128,1]{1,2,0:T(1,128)S(1)} %bitcast.96, f32[128,128]{1,0:T(8,128)S(1)} %get-tuple-element.140, f32[128,128]{1,0:T(8,128)S(1)} %get-tuple-element.141, pred[128,128]{1,0:T(8,128)(4,1)S(1)} %iota_compare_fusion.10), kind=kOutput, calls=%fused_computation.clone.1 | convolution fusion | flops 35651584 | bytes 278528 | tf_op jit(solution)/shard_map/while/body/eval_jaxpr/ts,tsc,sc->tc/dot_general | solution.py:30
  199.1 9.7 %fusion.104 = f32[128,1,128]{2,1,0:T(1,128)S(1)} fusion(f32[128,128,1]{1,2,0:T(1,128)S(1)} %bitcast.96, f32[128,128]{1,0:T(8,128)S(1)} %get-tuple-element.140, f32[128,128]{1,0:T(8,128)S(1)} %get-tuple-element.141, pred[128,128]{1,0:T(8,128)(4,1)S(1)} %iota_compare_fusion.10), kind=kOutput, calls=%fused_computation.clone.1 | convolution fusion | flops 35651584 | bytes 278528 | tf_op jit(solution)/shard_map/while/body/eval_jaxpr/ts,tsc,sc->tc/dot_general | solution.py:30
  208.9 9.7 %fusion.104 = f32[128,1,128]{2,1,0:T(1,128)S(1)} fusion(f32[128,128,1]{1,2,0:T(1,128)S(1)} %bitcast.96, f32[128,128]{1,0:T(8,128)S(1)} %get-tuple-element.140, f32[128,128]{1,0:T(8,128)S(1)} %get-tuple-element.141, pred[128,128]{1,0:T(8,128)(4,1)S(1)} %iota_compare_fusion.10), kind=kOutput, calls=%fused_computation.clone.1 | convolution fusion | flops 35651584 | bytes 278528 | tf_op jit(solution)/shard_map/while/body/eval_jaxpr/ts,tsc,sc->tc/dot_general | solution.py:30
  218.6 90.2 %while.21 = (s32[]{:T(128)}, f32[512,16]{0,1:T(8,128)S(1)}, f32[512]{0:T(512)S(1)}, f32[512,16]{0,1:T(8,128)S(1)}, s32[]{:T(128)}) while((s32[]{:T(128)}, f32[512,16]{0,1:T(8,128)S(1)}, f32[512]{0:T(512)S(1)}, f32[512,16]{0,1:T(8,128)S(1)}, s32[]{:T(128)}) %tuple.40), condition=%wide.region_4.5_spmd, body=%wide.region_3.4_spmd.sunk | while | flops 16386 | bytes 231525 | solution.py:100
  218.6 2.7 collective-permute-start
  221.3 1.0 collective-permute-done
  222.4 3.6 collective-permute-start
  227.0 3.6 collective-permute-start
  231.7 3.6 collective-permute-start
  235.3 1.0 collective-permute-done
  236.3 3.7 collective-permute-start
  241.1 5.9 collective-permute-start
  247.0 1.0 collective-permute-done
  248.0 5.6 collective-permute-start
  254.6 5.8 collective-permute-start
  261.4 5.8 collective-permute-start
  268.2 5.8 collective-permute-start
  274.9 5.8 collective-permute-start
  280.7 1.0 collective-permute-done
  281.7 5.8 collective-permute-start
  287.5 1.2 collective-permute-done
  288.6 5.6 collective-permute-start
  294.2 1.0 collective-permute-done
  295.3 5.8 collective-permute-start
  301.0 1.0 collective-permute-done
  302.0 5.8 collective-permute-start
  307.8 1.0 collective-permute-done
  309.3 3.9 convolution_convert_fusion.1
  313.9 81.5 %reduce-scatter.3.cloned.1.call-done = bf16[8,4096]{1,0:T(8,128)(2,1)} async-done(((bf16[128,4096]{1,0:T(8,128)(2,1)}), bf16[8,4096]{1,0:T(8,128)(2,1)}) %reduce-scatter.3.cloned.1.call-update) | async-done | bytes 65552 | tf_op jit(solution)/shard_map/reduce_scatter | solution.py:110
  396.9 19.3 %all_to_all.15 = bf16[16,2,4096]{2,1,0:T(2,128)(2,1)S(1)} all-to-all(bf16[16,2,4096]{2,1,0:T(2,128)(2,1)S(1)} %reshape.84), channel_id=1, replica_groups=mesh['ctx'=16,'exp'=16] {'exp'}, dimensions={0} | all-to-all | bytes 524288 | tf_op jit(solution)/shard_map/all_to_all | solution.py:144
  417.2 52.9 %all-gather.11.cloned.1.call-done = bf16[512,4096]{1,0:T(8,128)(2,1)} async-done(((bf16[32,4096]{1,0:T(8,128)(2,1)}), bf16[512,4096]{1,0:T(8,128)(2,1)}) %all-gather.11.cloned.1.call-update) | async-done | bytes 4194320 | tf_op jit(solution)/shard_map/all_gather | solution.py:149
  470.2 5.4 fusion.18
  475.6 10.8 %convolution_convert_fusion = bf16[512,4096]{1,0:T(8,128)(2,1)} fusion(bf16[1,448,4096]{2,1,0:T(8,128)(2,1)} %param.32, bf16[512,4096]{1,0:T(8,128)(2,1)} %all-gather.11.cloned.1.call-done, bf16[1,448,4096]{2,1,0:T(8,128)(2,1)} %param.31, f32[512,448]{0,1:T(8,128)S(1)} %fusion.18), kind=kOutput, calls=%fused_computation.19 | convolution fusion | flops 3761569792 | bytes 16646144 | tf_op jit(solution)/shard_map/dot_general | solution.py:157
  486.4 80.9 %reduce-scatter.5.cloned.1.call-done = bf16[32,4096]{1,0:T(8,128)(2,1)} async-done(((bf16[512,4096]{1,0:T(8,128)(2,1)}), bf16[32,4096]{1,0:T(8,128)(2,1)}) %reduce-scatter.5.cloned.1.call-update) | async-done | bytes 262160 | tf_op jit(solution)/shard_map/reduce_scatter | solution.py:158
  567.2 1.8 reshape.86
  569.1 9.4 %all-to-all-start.2 = ((bf16[16,2,4096]{2,1,0:T(2,128)(2,1)}), bf16[16,2,4096]{2,1,0:T(2,128)(2,1)S(1)}, u32[]{:S(2)}, u32[]{:S(2)}) async-start(bf16[16,2,4096]{2,1,0:T(2,128)(2,1)} %reshape.86), calls=%async_computation.4 | async-start | bytes 524288 | tf_op jit(solution)/shard_map/all_to_all | solution.py:161
  578.9 11.2 %all-to-all-done.2 = bf16[16,2,4096]{2,1,0:T(2,128)(2,1)S(1)} async-done(((bf16[16,2,4096]{2,1,0:T(2,128)(2,1)}), bf16[16,2,4096]{2,1,0:T(2,128)(2,1)S(1)}, u32[]{:S(2)}, u32[]{:S(2)}) %all-to-all-start.2) | async-done | bytes 262176 | tf_op jit(solution)/shard_map/all_to_all | solution.py:161
  (99 shorter events, 16.1 us)
Async XLA Ops:
  6.5 14.2 %copy-start = (f32[128,512]{1,0:T(8,128)S(1)}, f32[128,512]{1,0:T(8,128)}, u32[]{:S(2)}) copy-start(f32[128,512]{1,0:T(8,128)} %param.25) | copy-start | bytes 786436
  6.5 14.6 %copy-start.3 = (f32[4,512]{1,0:T(4,128)S(1)}, f32[4,512]{1,0:T(4,128)}, u32[]{:S(2)}) copy-start(f32[4,512]{1,0:T(4,128)} %param.22) | copy-start | bytes 24580
  6.5 63.6 %all-gather.5.cloned.1.call-start = ((), (), s32[]{:S(2)}) async-start(), calls=%async_computation.5 | async-start | bytes 4456448 | tf_op jit(solution)/shard_map/all_gather | solution.py:57
  7.3 121.7 %all-gather.7.cloned.1.call-start = ((), (), s32[]{:S(2)}) async-start(), calls=%async_computation.6 | async-start | bytes 4456448 | tf_op jit(solution)/shard_map/all_gather | solution.py:62
  10.0 37.9 %all-to-all-start = ((bf16[16,128,256]{2,1,0:T(8,128)(2,1)}), bf16[16,128,256]{2,1,0:T(8,128)(2,1)S(1)}, u32[]{:S(2)}, u32[]{:S(2)}) async-start(bf16[16,128,256]{2,1,0:T(8,128)(2,1)} %stack.2), calls=%async_computation | async-start | bytes 2097152 | tf_op jit(solution)/shard_map/all_to_all | solution.py:51
  20.0 289.3 %all-gather.9.cloned.1.call-start = ((), (), s32[]{:S(2)}) async-start(), calls=%async_computation.7 | async-start | bytes 4456448 | tf_op jit(solution)/shard_map/all_gather | solution.py:109
  20.7 374.7 %reduce-scatter.3.cloned.1.call-start = ((), (), s32[]{:S(2)}) async-start(), calls=%async_computation.8 | async-start | bytes 1114112 | tf_op jit(solution)/shard_map/reduce_scatter | solution.py:110
  73.1 58.8 %copy-start.5 = (f32[512]{0:T(512)S(1)}, f32[512]{0:T(512)}, u32[]{:S(2)}) copy-start(f32[512]{0:T(512)} %param.23) | copy-start | bytes 6148
  73.1 59.0 %copy-start.1 = (bf16[512,32]{0,1:T(8,128)(2,1)S(1)}, bf16[512,32]{0,1:T(8,128)(2,1)}, u32[]{:S(2)}) copy-start(bf16[512,32]{0,1:T(8,128)(2,1)} %param.24) | copy-start | bytes 98308
  73.1 58.7 %collective-permute-start.1 = (bf16[3,512]{1,0:T(4,128)(2,1)S(1)}, bf16[3,512]{1,0:T(4,128)(2,1)S(1)}, u32[]{:S(2)}, u32[]{:S(2)}) collective-permute-start(bf16[3,512]{1,0:T(4,128)(2,1)S(1)} %slice.48), channel_id=1, source_target_pairs={{0,16},{16,32},{32,48},{48,64},{64,80},{80,96},{96,112},{112,128},... | collective-permute-start | bytes 9224 | tf_op jit(solution)/shard_map/ppermute | solution.py:16
  179.5 129.3 %copy-start.7 = (f32[512]{0:T(512)S(1)}, f32[512]{0:T(512)}, u32[]{:S(2)}) copy-start(f32[512]{0:T(512)} %param.26) | copy-start | bytes 6148
  218.6 3.7 collective-permute-start
  222.4 4.7 collective-permute-start
  227.0 4.7 collective-permute-start
  231.7 4.7 collective-permute-start
  236.3 4.7 collective-permute-start
  241.1 6.9 %collective-permute-start = (f32[512,16]{0,1:T(8,128)S(1)}, f32[512,16]{0,1:T(8,128)S(1)}, u32[]{:S(2)}, u32[]{:S(2)}) collective-permute-start(f32[512,16]{0,1:T(8,128)S(1)} %multiply_add_fusion.3), channel_id=1, source_target_pairs={{0,16},{16,32},{32,48},{48,64},{64,80},{80,96},{96,112},{112,128},... | collective-permute-start | bytes 98312 | tf_op jit(solution)/shard_map/while/body/eval_jaxpr/ppermute | solution.py:16
  248.0 6.6 %collective-permute-start = (f32[512,16]{0,1:T(8,128)S(1)}, f32[512,16]{0,1:T(8,128)S(1)}, u32[]{:S(2)}, u32[]{:S(2)}) collective-permute-start(f32[512,16]{0,1:T(8,128)S(1)} %multiply_add_fusion.3), channel_id=1, source_target_pairs={{0,16},{16,32},{32,48},{48,64},{64,80},{80,96},{96,112},{112,128},... | collective-permute-start | bytes 98312 | tf_op jit(solution)/shard_map/while/body/eval_jaxpr/ppermute | solution.py:16
  254.6 6.8 %collective-permute-start = (f32[512,16]{0,1:T(8,128)S(1)}, f32[512,16]{0,1:T(8,128)S(1)}, u32[]{:S(2)}, u32[]{:S(2)}) collective-permute-start(f32[512,16]{0,1:T(8,128)S(1)} %multiply_add_fusion.3), channel_id=1, source_target_pairs={{0,16},{16,32},{32,48},{48,64},{64,80},{80,96},{96,112},{112,128},... | collective-permute-start | bytes 98312 | tf_op jit(solution)/shard_map/while/body/eval_jaxpr/ppermute | solution.py:16
  261.4 6.8 %collective-permute-start = (f32[512,16]{0,1:T(8,128)S(1)}, f32[512,16]{0,1:T(8,128)S(1)}, u32[]{:S(2)}, u32[]{:S(2)}) collective-permute-start(f32[512,16]{0,1:T(8,128)S(1)} %multiply_add_fusion.3), channel_id=1, source_target_pairs={{0,16},{16,32},{32,48},{48,64},{64,80},{80,96},{96,112},{112,128},... | collective-permute-start | bytes 98312 | tf_op jit(solution)/shard_map/while/body/eval_jaxpr/ppermute | solution.py:16
  268.2 6.8 %collective-permute-start = (f32[512,16]{0,1:T(8,128)S(1)}, f32[512,16]{0,1:T(8,128)S(1)}, u32[]{:S(2)}, u32[]{:S(2)}) collective-permute-start(f32[512,16]{0,1:T(8,128)S(1)} %multiply_add_fusion.3), channel_id=1, source_target_pairs={{0,16},{16,32},{32,48},{48,64},{64,80},{80,96},{96,112},{112,128},... | collective-permute-start | bytes 98312 | tf_op jit(solution)/shard_map/while/body/eval_jaxpr/ppermute | solution.py:16
  274.9 6.8 %collective-permute-start = (f32[512,16]{0,1:T(8,128)S(1)}, f32[512,16]{0,1:T(8,128)S(1)}, u32[]{:S(2)}, u32[]{:S(2)}) collective-permute-start(f32[512,16]{0,1:T(8,128)S(1)} %multiply_add_fusion.3), channel_id=1, source_target_pairs={{0,16},{16,32},{32,48},{48,64},{64,80},{80,96},{96,112},{112,128},... | collective-permute-start | bytes 98312 | tf_op jit(solution)/shard_map/while/body/eval_jaxpr/ppermute | solution.py:16
  281.7 6.9 %collective-permute-start = (f32[512,16]{0,1:T(8,128)S(1)}, f32[512,16]{0,1:T(8,128)S(1)}, u32[]{:S(2)}, u32[]{:S(2)}) collective-permute-start(f32[512,16]{0,1:T(8,128)S(1)} %multiply_add_fusion.3), channel_id=1, source_target_pairs={{0,16},{16,32},{32,48},{48,64},{64,80},{80,96},{96,112},{112,128},... | collective-permute-start | bytes 98312 | tf_op jit(solution)/shard_map/while/body/eval_jaxpr/ppermute | solution.py:16
  288.6 6.6 %collective-permute-start = (f32[512,16]{0,1:T(8,128)S(1)}, f32[512,16]{0,1:T(8,128)S(1)}, u32[]{:S(2)}, u32[]{:S(2)}) collective-permute-start(f32[512,16]{0,1:T(8,128)S(1)} %multiply_add_fusion.3), channel_id=1, source_target_pairs={{0,16},{16,32},{32,48},{48,64},{64,80},{80,96},{96,112},{112,128},... | collective-permute-start | bytes 98312 | tf_op jit(solution)/shard_map/while/body/eval_jaxpr/ppermute | solution.py:16
  295.3 6.8 %collective-permute-start = (f32[512,16]{0,1:T(8,128)S(1)}, f32[512,16]{0,1:T(8,128)S(1)}, u32[]{:S(2)}, u32[]{:S(2)}) collective-permute-start(f32[512,16]{0,1:T(8,128)S(1)} %multiply_add_fusion.3), channel_id=1, source_target_pairs={{0,16},{16,32},{32,48},{48,64},{64,80},{80,96},{96,112},{112,128},... | collective-permute-start | bytes 98312 | tf_op jit(solution)/shard_map/while/body/eval_jaxpr/ppermute | solution.py:16
  302.0 6.8 %collective-permute-start = (f32[512,16]{0,1:T(8,128)S(1)}, f32[512,16]{0,1:T(8,128)S(1)}, u32[]{:S(2)}, u32[]{:S(2)}) collective-permute-start(f32[512,16]{0,1:T(8,128)S(1)} %multiply_add_fusion.3), channel_id=1, source_target_pairs={{0,16},{16,32},{32,48},{48,64},{64,80},{80,96},{96,112},{112,128},... | collective-permute-start | bytes 98312 | tf_op jit(solution)/shard_map/while/body/eval_jaxpr/ppermute | solution.py:16
  308.8 4.5 copy-start.4
  308.8 87.6 %copy-start.2 = (f32[4096]{0:T(1024)S(1)}, f32[4096]{0:T(1024)}, u32[]{:S(2)}) copy-start(f32[4096]{0:T(1024)} %param.28) | copy-start | bytes 49156
  313.2 156.9 %all-gather.11.cloned.1.call-start = ((), (), s32[]{:S(2)}) async-start(), calls=%async_computation.9 | async-start | bytes 4456448 | tf_op jit(solution)/shard_map/all_gather | solution.py:149
  417.0 150.2 %reduce-scatter.5.cloned.1.call-start = ((), (), s32[]{:S(2)}) async-start(), calls=%async_computation.10 | async-start | bytes 4456448 | tf_op jit(solution)/shard_map/reduce_scatter | solution.py:158
  486.3 92.1 %copy-start.6 = (bf16[4096,16]{0,1:T(8,128)(2,1)S(1)}, bf16[4096,16]{0,1:T(8,128)(2,1)}, u32[]{:S(2)}) copy-start(bf16[4096,16]{0,1:T(8,128)(2,1)} %param.29) | copy-start | bytes 393220
  569.1 21.1 %all-to-all-start.2 = ((bf16[16,2,4096]{2,1,0:T(2,128)(2,1)}), bf16[16,2,4096]{2,1,0:T(2,128)(2,1)S(1)}, u32[]{:S(2)}, u32[]{:S(2)}) async-start(bf16[16,2,4096]{2,1,0:T(2,128)(2,1)} %reshape.86), calls=%async_computation.4 | async-start | bytes 524288 | tf_op jit(solution)/shard_map/all_to_all | solution.py:161
Sparse Core Ops, SparseCore 0:
  9.8 60.3 all-gather.4
  72.6 56.2 all-gather.6
  131.3 61.4 all-gather.8
  313.4 82.0 reduce-scatter.2
  417.1 52.9 all-gather.10
  486.5 80.7 reduce-scatter.4
